TPU v7x, 32 devices: a whole 2x2x4 slice. The times are simulated.
32 devices in a mesh: wide: 4 (over z), narrow: 8 (over y, x, core).
Axes of the slice: x: 2, y: 2, z: 4, core: 2. Of those that a mesh axis runs over, the one named last changes fastest.
Arguments:
- layer_entry_input: bfloat16 [4096, 2048], P('wide'), may hold values from -6 to 6
- ln1_gain: float32 [2048], replicated, may hold values from 0.5 to 1.5
- ln1_bias: float32 [2048], replicated, may hold values from -1 to 1
- w_qkv: bfloat16 [2048, 3, 2048], P(None, None, 'narrow'), may hold values from -0.125 to 0.125
- b_qv: float32 [2, 2048], P(None, 'narrow'), may hold values from -1.5 to 1.5
- w_out: bfloat16 [2048, 2048], P('narrow'), may hold values from -2 to 2
- b_out: float32 [2048], replicated, may hold values from -1.5 to 1.5
- ln2_gain: float32 [2048], replicated, may hold values from 0.5 to 1.5
- ln2_bias: float32 [2048], replicated, may hold values from -1 to 1
- w_up: bfloat16 [2048, 8192], P(None, 'narrow'), may hold values from -0.125 to 0.125
- b_up: float32 [8192], P('narrow'), may hold values from -2.5 to 2.5
- w_down: bfloat16 [8192, 2048], P('narrow'), may hold values from -0.0625 to 0.0625
- b_down: float32 [2048], replicated, may hold values from -1.5 to 1.5
- document_index: int32 [4096], replicated, may hold values from 0 to 8, as said below
- positions: int32 [4096], replicated, may hold values from 0 to 767, as said below
- valid: int32 [4096], replicated, may hold values from 0 to 1, as said below
- cotangent: bfloat16 [4096, 2048], P('wide'), may hold values from -6 to 6
Outputs:
- output: bfloat16 [4096, 2048], P('wide')
- grad_input: bfloat16 [4096, 2048], P('wide')
- grad_ln1_gain: float32 [2048], replicated
- grad_ln1_bias: float32 [2048], replicated
- grad_w_qkv: float32 [2048, 3, 2048], P(None, None, 'narrow')
- grad_b_qv: float32 [2, 2048], P(None, 'narrow')
- grad_w_out: float32 [2048, 2048], P('narrow')
- grad_b_out: float32 [2048], replicated
- grad_ln2_gain: float32 [2048], replicated
- grad_ln2_bias: float32 [2048], replicated
- grad_w_up: float32 [2048, 8192], P(None, 'narrow')
- grad_b_up: float32 [8192], P('narrow')
- grad_w_down: float32 [8192, 2048], P('narrow')
- grad_b_down: float32 [2048], replicated
Inputs may be any that keep to these rules, and one draw needn't show every extreme that they name: `document_index`: documents are contiguous and numbered in order from 0; each block of 1024 tokens of one index of wide holds exactly two document starts, and every document has at most 768 tokens. `positions`: counts from 0 at the first token of each document, padding included. `valid`: 0 exactly on the last 1 to 64 tokens of each document.
All inputs are finite; a program needn't handle non-finite values.
Results may differ from a plain program's by a relative error of at most 0.019.
Values may be sent and summed in bfloat16 or wider, within the bound.
No kernel may reach another device: no remote copies, remote signals or barrier semaphores. Data moves between devices by JAX's collectives and lax.ppermute only.
A program may use at most 192 MiB of HBM per device.

v0:
```python
import jax
import jax.numpy as jnp
from jax import lax
from jax.sharding import PartitionSpec as P

HEAD_DIM = 128
ROW_TOKENS = 2048


def from_behind(value, axis, steps):
    count = lax.axis_size(axis)
    initial, last = (max(0, -steps), min(count, count - steps))
    return lax.ppermute(value, axis, [(source, source + steps) for source in range(initial, last)])


def norm_stats(values):
    center = values - jnp.mean(values, axis=-1, keepdims=True)
    spread = jnp.mean(center * center, axis=-1, keepdims=True)
    inverse = lax.rsqrt(spread + 1e-05)
    return (center * inverse, inverse)


def norm_local(grad_out, normed_raw, inverse, gain):
    scaled = grad_out * gain
    grad_in = inverse * (
        scaled
        - jnp.mean(scaled, axis=-1, keepdims=True)
        - normed_raw * jnp.mean(scaled * normed_raw, axis=-1, keepdims=True)
    )
    return (grad_in, jnp.sum(grad_out * normed_raw, axis=0), jnp.sum(grad_out, axis=0))


def norm_back(partial_value, normed_raw, inverse, gain):
    summed = lax.psum(partial_value, "narrow")
    return norm_local(summed, normed_raw, inverse, gain)


def on_device(
    layer_entry_input,
    ln1_gain,
    ln1_bias,
    w_qkv,
    b_qv,
    w_out,
    b_out,
    ln2_gain,
    ln2_bias,
    w_up,
    b_up,
    w_down,
    b_down,
    document_index,
    positions,
    valid,
    cotangent,
):
    token_rows = layer_entry_input.shape[0]
    local_width = w_qkv.shape[2]
    head_count = local_width // HEAD_DIM
    document_spans = ROW_TOKENS // token_rows
    key_rows = document_spans * token_rows
    scale = HEAD_DIM ** (-0.5)
    start = lax.axis_index("wide") * token_rows
    query_index = start + jnp.arange(token_rows, dtype=jnp.int32)
    key_index = start - (document_spans - 1) * token_rows + jnp.arange(key_rows, dtype=jnp.int32)
    safe_index = jnp.clip(key_index, 0, document_index.shape[0] - 1)
    seg_query = lax.dynamic_slice_in_dim(document_index, start, token_rows, 0)
    pos_query = lax.dynamic_slice_in_dim(positions, start, token_rows, 0)
    seg_key = jnp.take(document_index, safe_index)
    pos_key = jnp.take(positions, safe_index)
    valid_key = jnp.take(valid, safe_index)
    allowed = (
        (key_index[None, :] >= 0)
        & (seg_key[None, :] == seg_query[:, None])
        & (pos_key[None, :] <= pos_query[:, None])
        & ((valid_key[None, :] == 1) | (key_index[None, :] == query_index[:, None]))
    )
    inputs = layer_entry_input.astype(jnp.float32)
    raw_one, inv_one = norm_stats(inputs)
    normed_one = (raw_one * ln1_gain + ln1_bias).astype(jnp.bfloat16)
    mixed = jnp.einsum("td,dch->tch", normed_one, w_qkv, preferred_element_type=jnp.float32)
    query = (mixed[:, 0] + b_qv[0]).astype(jnp.bfloat16)
    key_val = jnp.stack([mixed[:, 1], mixed[:, 2] + b_qv[1]]).astype(jnp.bfloat16)
    pieces = [key_val]
    current = key_val
    current = from_behind(current, "wide", 1)
    pieces.insert(0, current)
    joined = jnp.concatenate(pieces, axis=1)
    keys_heads = joined[0].reshape(key_rows, head_count, HEAD_DIM)
    vals_heads = joined[1].reshape(key_rows, head_count, HEAD_DIM)
    query_heads = query.reshape(token_rows, head_count, HEAD_DIM)

    def scores_of():
        raw = (
            jnp.einsum("qhd,khd->hqk", query_heads, keys_heads, preferred_element_type=jnp.float32)
            * scale
        )
        return jnp.where(allowed[None], raw, -1e30)

    scores = scores_of()
    row_max = jnp.max(scores, axis=-1, keepdims=True)
    log_total = row_max + jnp.log(jnp.sum(jnp.exp(scores - row_max), axis=-1, keepdims=True))
    probs = jnp.exp(scores - log_total)
    attended = jnp.einsum(
        "hqk,khd->qhd", probs.astype(jnp.bfloat16), vals_heads, preferred_element_type=jnp.float32
    )
    attended = attended.reshape(token_rows, local_width).astype(jnp.bfloat16)
    attn_total = lax.psum(
        jnp.dot(attended, w_out, preferred_element_type=jnp.float32).astype(jnp.bfloat16), "narrow"
    ).astype(jnp.float32)
    after_attn = inputs + b_out + attn_total
    raw_two, inv_two = norm_stats(after_attn)
    normed_two = (raw_two * ln2_gain + ln2_bias).astype(jnp.bfloat16)
    upper = jnp.dot(normed_two, w_up, preferred_element_type=jnp.float32) + b_up
    active, gelu_pull = jax.vjp(jax.nn.gelu, upper)
    active = active.astype(jnp.bfloat16)
    mlp_total = lax.psum(
        jnp.dot(active, w_down, preferred_element_type=jnp.float32).astype(jnp.bfloat16), "narrow"
    ).astype(jnp.float32)
    output = (after_attn + b_down + mlp_total).astype(jnp.bfloat16)
    grad_out = cotangent.astype(jnp.float32)
    grad_b_down = jnp.sum(grad_out, axis=0)
    grad_w_down = jnp.einsum("tf,td->fd", active, cotangent, preferred_element_type=jnp.float32)
    grad_active = jnp.einsum("td,fd->tf", cotangent, w_down, preferred_element_type=jnp.float32)
    grad_upper = gelu_pull(grad_active)[0].astype(jnp.bfloat16)
    grad_w_up = jnp.einsum("td,tf->df", normed_two, grad_upper, preferred_element_type=jnp.float32)
    grad_b_up = jnp.sum(grad_upper.astype(jnp.float32), axis=0)
    grad_norm_two = jnp.einsum("tf,df->td", grad_upper, w_up, preferred_element_type=jnp.float32)
    grad_resid_two, grad_ln2_gain, grad_ln2_bias = norm_back(
        grad_norm_two, raw_two, inv_two, ln2_gain
    )
    grad_mid = grad_out + grad_resid_two
    grad_b_out = jnp.sum(grad_mid, axis=0)
    grad_mid_low = grad_mid.astype(jnp.bfloat16)
    grad_w_out = jnp.einsum("th,td->hd", attended, grad_mid_low, preferred_element_type=jnp.float32)
    grad_attended = jnp.einsum(
        "td,hd->th", grad_mid_low, w_out, preferred_element_type=jnp.float32
    ).astype(jnp.bfloat16)
    grad_att_heads = grad_attended.reshape(token_rows, head_count, HEAD_DIM)
    probs_again = jnp.exp(scores_of() - log_total)
    grad_vals = jnp.einsum(
        "hqk,qhd->khd",
        probs_again.astype(jnp.bfloat16),
        grad_att_heads,
        preferred_element_type=jnp.float32,
    )
    grad_probs = jnp.einsum(
        "qhd,khd->hqk", grad_att_heads, vals_heads, preferred_element_type=jnp.float32
    )
    grad_scores = (
        probs_again * (grad_probs - jnp.sum(probs_again * grad_probs, axis=-1, keepdims=True))
    ).astype(jnp.bfloat16)
    grad_query = (
        jnp.einsum("hqk,khd->qhd", grad_scores, keys_heads, preferred_element_type=jnp.float32)
        * scale
    )
    grad_keys = (
        jnp.einsum("hqk,qhd->khd", grad_scores, query_heads, preferred_element_type=jnp.float32)
        * scale
    )
    grad_kv = jnp.stack([grad_keys, grad_vals]).reshape(2, document_spans, token_rows, local_width)
    carried = grad_kv[:, 0]
    carried = from_behind(carried, "wide", -1)
    carried = carried + grad_kv[:, 1]
    grad_mixed = jnp.stack(
        [grad_query.reshape(token_rows, local_width), carried[0], carried[1]], axis=1
    ).astype(jnp.bfloat16)
    grad_w_qkv = jnp.einsum(
        "td,tch->dch", normed_one, grad_mixed, preferred_element_type=jnp.float32
    )
    mixed_sums = jnp.sum(grad_mixed.astype(jnp.float32), axis=0)
    grad_b_qv = jnp.stack([mixed_sums[0], mixed_sums[2]])
    grad_norm_one = jnp.einsum("tch,dch->td", grad_mixed, w_qkv, preferred_element_type=jnp.float32)
    grad_resid_one, grad_ln1_gain, grad_ln1_bias = norm_back(
        grad_norm_one, raw_one, inv_one, ln1_gain
    )
    grad_input = (grad_mid + grad_resid_one).astype(jnp.bfloat16)
    (
        grad_ln1_gain,
        grad_ln1_bias,
        grad_w_qkv,
        grad_b_qv,
        grad_w_out,
        grad_b_out,
        grad_ln2_gain,
        grad_ln2_bias,
        grad_w_up,
        grad_b_up,
        grad_w_down,
        grad_b_down,
    ) = lax.psum(
        (
            grad_ln1_gain,
            grad_ln1_bias,
            grad_w_qkv,
            grad_b_qv,
            grad_w_out,
            grad_b_out,
            grad_ln2_gain,
            grad_ln2_bias,
            grad_w_up,
            grad_b_up,
            grad_w_down,
            grad_b_down,
        ),
        "wide",
    )
    return (
        output,
        grad_input,
        grad_ln1_gain,
        grad_ln1_bias,
        grad_w_qkv,
        grad_b_qv,
        grad_w_out,
        grad_b_out,
        grad_ln2_gain,
        grad_ln2_bias,
        grad_w_up,
        grad_b_up,
        grad_w_down,
        grad_b_down,
    )


def solution(mesh):
    return jax.shard_map(
        on_device,
        mesh=mesh,
        in_specs=(
            P("wide", None),
            P(),
            P(),
            P(None, None, "narrow"),
            P(None, "narrow"),
            P("narrow", None),
            P(),
            P(),
            P(),
            P(None, "narrow"),
            P("narrow"),
            P("narrow", None),
            P(),
            P(),
            P(),
            P(),
            P("wide", None),
        ),
        out_specs=(
            P("wide", None),
            P("wide", None),
            P(),
            P(),
            P(None, None, "narrow"),
            P(None, "narrow"),
            P("narrow", None),
            P(),
            P(),
            P(),
            P(None, "narrow"),
            P("narrow"),
            P("narrow", None),
            P(),
        ),
        check_vma=False,
    )
```

profile of v0, /device:TPU:0, one launch (start us, length us, event | category | flops | bytes accessed | tf_op | source)
XLA Modules:
  0.0 1541.9 jit_solution(12492880103837359195)
XLA Ops:
  18.7 6.4 collective-permute-start
  25.2 11.8 gather_fusion
  37.0 11.8 gather_fusion.2
  48.8 11.8 gather_fusion.1
  74.0 5.2 exponential_reduce_fusion
  79.9 6.6 convolution_convert_fusion.2
  86.5 4.7 convolution_convert_fusion
  91.3 80.2 %all-reduce.8.cloned.1.call-done = bf16[1024,2048]{1,0:T(8,128)(2,1)} async-done(((bf16[1024,2048]{1,0:T(8,128)(2,1)}), bf16[1024,2048]{1,0:T(8,128)(2,1)}) %all-reduce.8.cloned.1.call-update) | async-done | bytes 4194320 | tf_op jit(solution)/shard_map/psum | solution.py:108
  171.5 5.0 fusion.27
  189.6 7.3 convert_reduce_fusion.2
  198.2 6.8 fusion.60
  205.5 10.5 convolution_convert_fusion.1
  216.0 115.4 %all-reduce.12.cloned.1.call-done = f32[1024,2048]{1,0:T(8,128)} async-done(((f32[1024,2048]{1,0:T(8,128)}), f32[1024,2048]{1,0:T(8,128)}) %all-reduce.12.cloned.1.call-update) | async-done | bytes 8388624 | tf_op jit(solution)/shard_map/psum | solution.py:34
  331.4 8.5 multiply_reduce_fusion.1
  339.9 76.3 %all-reduce.10.cloned.1.call-done = bf16[1024,2048]{1,0:T(8,128)(2,1)} async-done(((bf16[1024,2048]{1,0:T(8,128)(2,1)}), bf16[1024,2048]{1,0:T(8,128)(2,1)}) %all-reduce.10.cloned.1.call-update) | async-done | bytes 4194320 | tf_op jit(solution)/shard_map/psum | solution.py:117
  416.2 13.9 fusion.55
  434.4 12.9 multiply_reduce_fusion
  447.3 10.1 convolution_bitcast_fusion.1
  457.3 12.4 multiply_convert_fusion
  496.5 7.1 fusion.37
  505.6 38.9 %collective-permute-done.1 = f32[2,1024,256]{2,1,0:T(8,128)} collective-permute-done((f32[2,1024,256]{2,1,0:T(8,128)}, f32[2,1024,256]{2,1,0:T(8,128)}, u32[]{:S(2)}, u32[]{:S(2)}) %collective-permute-start.1) | collective-permute-done | bytes 2097184 | tf_op jit(solution)/shard_map/ppermute | solution.py:13
  548.0 5.7 convolution_bitcast_fusion
  553.8 10.8 fusion.61
  564.6 7.6 fusion.53
  572.3 6.4 fusion.33
  578.8 6.9 fusion.41
  587.4 91.9 %all-reduce.14.cloned.1.call-done = f32[1024,2048]{1,0:T(8,128)} async-done(((f32[1024,2048]{1,0:T(8,128)}), f32[1024,2048]{1,0:T(8,128)}) %all-reduce.14.cloned.1.call-update) | async-done | bytes 8388624 | tf_op jit(solution)/shard_map/psum | solution.py:34
  679.3 6.5 fusion.15
  685.9 28.7 %all-reduce = (f32[2048]{0:T(1024)}, f32[2048]{0:T(1024)}, f32[2,256]{1,0:T(2,128)}, f32[2048]{0:T(1024)}, f32[2048]{0:T(1024)}, /*index=5*/f32[2048]{0:T(1024)}, f32[1024]{0:T(1024)}, f32[2048]{0:T(1024)}) all-reduce(f32[2048]{0:T(1024)S(1)} %get-tuple-element.17, ...), channel_id=1, replica_groups=mesh['wide'=4,'narrow'=8] {'wide'}, use_global_device_ids=true, to_apply=%region_16.18 | all-reduce | flops 13824 | bytes 110592 | tf_op jit(solution)/shard_map/psum | solution.py:191
  714.6 10.7 fusion.14
  725.3 792.0 %all-reduce.16.cloned.1.call-done = (f32[2048,3,256]{2,0,1:T(8,128)}, f32[256,2048]{1,0:T(8,128)}, f32[2048,1024]{1,0:T(8,128)}, f32[1024,2048]{1,0:T(8,128)}) async-done(((f32[2048,3,256]{2,0,1:T(8,128)}, f32[256,2048]{1,0:T(8,128)}, f32[2048,1024]{1,0:T(8,128)}, f32[1024,2048]{1,0:T(8,128)}), (f32[2048,3,256]{2,0,1:T(8,128)}, f32[256,2048]{1,0:T(8,128)}, f32[2048,1024]{1,0:T(8,128)}, ...) | async-done | bytes 25165840 | tf_op jit(solution)/shard_map/psum | solution.py:191
  1517.3 6.6 copy.64
  (176 shorter events, 89.7 us)
Async XLA Ops:
  7.2 164.2 %all-reduce.8.cloned.1.call-start = ((), (), s32[]{:S(2)}) async-start(), calls=%async_computation | async-start | bytes 8388608 | tf_op jit(solution)/shard_map/psum | solution.py:108
  16.3 8.8 copy-start.29
  16.3 8.8 copy-start.2
  18.7 47.7 %collective-permute-start = (bf16[2,1024,256]{1,2,0:T(8,128)(2,1)}, bf16[2,1024,256]{1,2,0:T(8,128)(2,1)}, u32[]{:S(2)}, u32[]{:S(2)}) collective-permute-start(bf16[2,1024,256]{1,2,0:T(8,128)(2,1)} %pad_maximum_fusion.2), channel_id=1, source_target_pairs={{0,8},{8,16},{16,24},{1,9},{9,17},{17,25},{2,10},{10,18},{18,26},{... | collective-permute-start | bytes 3145736 | tf_op jit(solution)/shard_map/ppermute | solution.py:13
  25.1 11.8 copy-start.3
  37.0 11.8 copy-start.1
  62.1 11.8 copy-start.13
  66.4 7.6 copy-start.11
  86.5 85.0 %copy-start.37 = (f32[2048]{0:T(1024)S(1)}, f32[2048]{0:T(1024)}, u32[]{:S(2)}) copy-start(f32[2048]{0:T(1024)} %param.25) | copy-start | bytes 24580
  91.2 240.2 %all-reduce.12.cloned.1.call-start = ((), (), s32[]{:S(2)}) async-start(), calls=%async_computation.2 | async-start | bytes 16777216 | tf_op jit(solution)/shard_map/psum | solution.py:34
  189.6 7.3 copy-start.53
  205.0 211.2 %all-reduce.10.cloned.1.call-start = ((), (), s32[]{:S(2)}) async-start(), calls=%async_computation.1 | async-start | bytes 8388608 | tf_op jit(solution)/shard_map/psum | solution.py:117
  215.9 200.3 %copy-start.46 = (f32[2048]{0:T(1024)S(1)}, f32[2048]{0:T(1024)}, u32[]{:S(2)}) copy-start(f32[2048]{0:T(1024)} %param.31) | copy-start | bytes 24580
  215.9 463.4 %all-reduce.14.cloned.1.call-start = ((), (), s32[]{:S(2)}) async-start(), calls=%async_computation.3 | async-start | bytes 16777216 | tf_op jit(solution)/shard_map/psum | solution.py:34
  416.2 13.9 copy-start.25
  457.3 15.8 %copy-start.14 = (f32[1024,1,256]{0,2,1:T(8,128)S(1)}, f32[1024,1,256]{0,2,1:T(8,128)}, u32[]{:S(2)}) copy-start(f32[1024,1,256]{0,2,1:T(8,128)} %copy-done.13) | copy-start | bytes 3145732
  495.2 49.3 %collective-permute-start.1 = (f32[2,1024,256]{2,1,0:T(8,128)}, f32[2,1024,256]{2,1,0:T(8,128)}, u32[]{:S(2)}, u32[]{:S(2)}) collective-permute-start(f32[2,1024,256]{2,1,0:T(8,128)} %fusion.29), channel_id=1, source_target_pairs={{8,0},{16,8},{24,16},{9,1},{17,9},{25,17},{10,2},{18,10},{26,18},{... | collective-permute-start | bytes 6291464 | tf_op jit(solution)/shard_map/ppermute | solution.py:13
  505.6 42.4 %copy-start.30 = (bf16[1024,1,256]{2,0,1:T(8,128)(2,1)S(1)}, bf16[1024,1,256]{2,0,1:T(8,128)(2,1)}, u32[]{:S(2)}) copy-start(bf16[1024,1,256]{2,0,1:T(8,128)(2,1)} %copy.47) | copy-start | bytes 1572868
  553.7 963.6 %all-reduce.16.cloned.1.call-start = ((), (), s32[]{:S(2)}) async-start(), calls=%async_computation.4 | async-start | bytes 50331648 | tf_op jit(solution)/shard_map/psum | solution.py:191
  553.8 10.8 copy-start.27
  553.8 10.8 copy-start.54
  564.6 7.6 copy-start.28
  572.2 6.5 copy-start.6
  572.2 6.5 copy-start.31
  572.2 6.5 copy-start.34
  572.2 6.5 copy-start.36
  572.3 6.5 copy-start.40
  572.3 6.5 copy-start.42
  572.3 6.5 copy-start.44
  1517.3 6.6 copy-start.32
  1517.3 8.9 copy-start.15
  1523.8 6.6 slice-start
  (33 other events, 134.7 us)
Sparse Core Ops, SparseCore 0:
  91.4 80.0 all-reduce.7
  205.1 126.2 all-reduce.11
  335.3 80.9 all-reduce.9
  553.8 125.4 all-reduce.13
  682.6 834.5 all-reduce.15
where the time goes:
time: 1550 us; the launch traced here: 1540 us
  waiting for transfers between devices  1190 us (77%)
  matrix products  120 us (8%)
  local copies, waits for them, and re-layouts  87.9 us (6%)
  other arithmetic  87 us (6%)
  blocking collectives  28.7 us (2%)
    psum x1, waiting for transfers between devices, on_device(): lax.psum((grad_ln1_gain, grad_ln1_bias, grad_w_qkv, grad_b_qv, grad_w_out...  792 us
    psum x2, waiting for transfers between devices, norm_back(): summed = lax.psum(partial_value, 'narrow')  207 us
    psum x1, waiting for transfers between devices, on_device(): lax.psum(jnp.dot(attended, w_out, preferred_element_type=jnp.float32).ast...  80.2 us
    psum x1, waiting for transfers between devices, on_device(): lax.psum(jnp.dot(active, w_down, preferred_element_type=jnp.float32).asty...  76.3 us
    ppermute x2, waiting for transfers between devices, from_behind(): lax.ppermute(value, axis, [(source, source + steps) for source in range(i...  38.9 us
    unnamed x120, local copies, waits for them, and re-layouts  31.5 us
  transfers between devices with their start and end apart: 7, of which 6 were waited for; matrix products, arithmetic and copies ran while one was open for 8% of the time, Pallas kernels for 0%

commit v1 on v0

--- a/solution.py
+++ b/solution.py
@@ -31,7 +31,9 @@
 
 
 def norm_back(partial_value, normed_raw, inverse, gain):
-    summed = lax.psum(partial_value, "narrow")
+    summed = partial_value
+    for hop in (1, 2, 4):
+        summed = summed + lax.ppermute(summed, "narrow", [(dev, dev ^ hop) for dev in range(8)])
     return norm_local(summed, normed_raw, inverse, gain)
 
 

time: 1550 us -> 1680 us (1.084)
  waiting for transfers between devices: 1190 us -> 1290 us
  other arithmetic: 87 us -> 144 us
    ppermute x0 -> x6, waiting for transfers between devices: none -> 773 us  [norm_back(): lax.ppermute(summed, 'narrow', [(dev, dev ^ hop) for dev in range(8)])]
    psum x1, waiting for transfers between devices: 792 us -> 401 us  [on_device(): lax.psum((grad_ln1_gain, grad_ln1_bias, grad_w_qkv, grad_b_qv, grad_w_out...]
    psum x2 -> x0, waiting for transfers between devices: 207 us -> none  [norm_back(): summed = lax.psum(partial_value, 'narrow')]
    psum x1, waiting for transfers between devices: 76.3 us -> 0.02 us  [on_device(): lax.psum(jnp.dot(active, w_down, preferred_element_type=jnp.float32).asty...]
    add x0 -> x4, other arithmetic: none -> 48.6 us  [norm_back(): summed + lax.ppermute(summed, 'narrow', [(dev, dev ^ hop) for dev in rang...]
  transfers between devices with their start and end apart: 7 -> 11, of which waited for: 6 -> 8; matrix products, arithmetic and copies ran while one was open for 8% -> 9% of each run, Pallas kernels for 0% -> 0%
where the time goes in v1:
time: 1680 us
  waiting for transfers between devices  1290 us (77%)
  other arithmetic  144 us (9%)
  matrix products  111 us (7%)
  local copies, waits for them, and re-layouts  89.1 us (5%)
  blocking collectives  20.6 us (1%)
    ppermute x6, waiting for transfers between devices, norm_back(): lax.ppermute(summed, 'narrow', [(dev, dev ^ hop) for dev in range(8)])  773 us
    psum x1, waiting for transfers between devices, on_device(): lax.psum((grad_ln1_gain, grad_ln1_bias, grad_w_qkv, grad_b_qv, grad_w_out...  401 us
    psum x1, waiting for transfers between devices, on_device(): lax.psum(jnp.dot(attended, w_out, preferred_element_type=jnp.float32).ast...  80 us
    add x4, other arithmetic, norm_back(): summed + lax.ppermute(summed, 'narrow', [(dev, dev ^ hop) for dev in rang...  48.6 us
  transfers between devices with their start and end apart: 11, of which 8 were waited for; matrix products, arithmetic and copies ran while one was open for 9% of the time, Pallas kernels for 0%

profile of v1, /device:TPU:0, one launch (start us, length us, event | category | flops | bytes accessed | tf_op | source)
XLA Modules:
  0.0 1676.9 jit_solution(13515087016918853114)
XLA Ops:
  18.7 6.1 collective-permute-start
  24.8 11.8 gather_fusion
  36.6 11.8 gather_fusion.2
  48.5 11.8 gather_fusion.1
  79.5 6.6 convolution_convert_fusion.2
  91.1 80.0 %all-reduce.6.cloned.1.call-done = bf16[1024,2048]{1,0:T(8,128)(2,1)} async-done(((bf16[1024,2048]{1,0:T(8,128)(2,1)}), bf16[1024,2048]{1,0:T(8,128)(2,1)}) %all-reduce.6.cloned.1.call-update) | async-done | bytes 4194320 | tf_op jit(solution)/shard_map/psum | solution.py:110
  189.0 7.9 convert_reduce_fusion.2
  204.9 13.3 collective-permute-done.1
  218.2 11.9 add.222
  231.5 181.3 %collective-permute-done.2 = f32[1024,2048]{1,0:T(8,128)} collective-permute-done((f32[1024,2048]{1,0:T(8,128)}, f32[1024,2048]{1,0:T(8,128)}, u32[]{:S(2)}, u32[]{:S(2)}) %collective-permute-start.2) | collective-permute-done | bytes 8388640 | tf_op jit(solution)/shard_map/ppermute | solution.py:36
  412.9 11.9 add.223
  426.1 10.5 convolution_convert_fusion.1
  436.6 215.0 %collective-permute-done.3 = f32[1024,2048]{1,0:T(8,128)} collective-permute-done((f32[1024,2048]{1,0:T(8,128)}, f32[1024,2048]{1,0:T(8,128)}, u32[]{:S(2)}, u32[]{:S(2)}) %collective-permute-start.3) | collective-permute-done | bytes 8388640 | tf_op jit(solution)/shard_map/ppermute | solution.py:36
  651.6 13.3 multiply_reduce_fusion.1
  665.0 13.9 fusion.55
  683.1 12.9 multiply_reduce_fusion
  696.0 10.2 convolution_bitcast_fusion.1
  706.2 12.2 multiply_convert_fusion
  745.5 9.5 fusion.61
  760.7 31.6 %collective-permute-done.4 = f32[2,1024,256]{2,1,0:T(8,128)} collective-permute-done((f32[2,1024,256]{2,1,0:T(8,128)}, f32[2,1024,256]{2,1,0:T(8,128)}, u32[]{:S(2)}, u32[]{:S(2)}) %collective-permute-start.4) | collective-permute-done | bytes 2097184 | tf_op jit(solution)/shard_map/ppermute | solution.py:13
  795.1 6.0 convolution_bitcast_fusion
  801.1 7.5 fusion.53
  811.3 7.1 fusion.41
  818.5 12.9 add.227
  832.5 182.2 %collective-permute-done.6 = f32[1024,2048]{1,0:T(8,128)} collective-permute-done((f32[1024,2048]{1,0:T(8,128)}, f32[1024,2048]{1,0:T(8,128)}, u32[]{:S(2)}, u32[]{:S(2)}) %collective-permute-start.6) | collective-permute-done | bytes 8388640 | tf_op jit(solution)/shard_map/ppermute | solution.py:36
  1014.7 12.0 add.228
  1028.1 180.8 %collective-permute-done.7 = f32[1024,2048]{1,0:T(8,128)S(1)} collective-permute-done((f32[1024,2048]{1,0:T(8,128)}, f32[1024,2048]{1,0:T(8,128)S(1)}, u32[]{:S(2)}, u32[]{:S(2)}) %collective-permute-start.7) | collective-permute-done | bytes 8388640 | tf_op jit(solution)/shard_map/ppermute | solution.py:36
  1208.9 9.9 fusion.15
  1218.8 20.6 %all-reduce = (f32[2048]{0:T(1024)}, f32[2048]{0:T(1024)}, f32[2,256]{1,0:T(2,128)}, f32[2048]{0:T(1024)}, f32[2048]{0:T(1024)}, /*index=5*/f32[2048]{0:T(1024)}, f32[1024]{0:T(1024)}, f32[2048]{0:T(1024)}) all-reduce(f32[2048]{0:T(1024)S(1)} %get-tuple-element.17, ...), channel_id=1, replica_groups=mesh['wide'=4,'narrow'=8] {'wide'}, use_global_device_ids=true, to_apply=%region_14.16 | all-reduce | flops 13824 | bytes 110592 | tf_op jit(solution)/shard_map/psum | solution.py:193
  1239.5 12.1 fusion.14
  1251.6 400.7 %all-reduce.10.cloned.1.call-done = (f32[2048,3,256]{2,0,1:T(8,128)}, f32[256,2048]{1,0:T(8,128)}, f32[2048,1024]{1,0:T(8,128)}, f32[1024,2048]{1,0:T(8,128)}) async-done(((f32[2048,3,256]{2,0,1:T(8,128)}, f32[256,2048]{1,0:T(8,128)}, f32[2048,1024]{1,0:T(8,128)}, f32[1024,2048]{1,0:T(8,128)}), (f32[2048,3,256]{2,0,1:T(8,128)}, f32[256,2048]{1,0:T(8,128)}, f32[2048,1024]{1,0:T(8,128)}, ...) | async-done | bytes 25165840 | tf_op jit(solution)/shard_map/psum | solution.py:193
  1652.3 6.6 copy.62
  (202 shorter events, 120.3 us)
Async XLA Ops:
  7.2 163.9 %all-reduce.6.cloned.1.call-start = ((), (), s32[]{:S(2)}) async-start(), calls=%async_computation | async-start | bytes 8388608 | tf_op jit(solution)/shard_map/psum | solution.py:110
  16.3 8.5 copy-start.2
  18.7 47.4 %collective-permute-start = (bf16[2,1024,256]{1,2,0:T(8,128)(2,1)}, bf16[2,1024,256]{1,2,0:T(8,128)(2,1)}, u32[]{:S(2)}, u32[]{:S(2)}) collective-permute-start(bf16[2,1024,256]{1,2,0:T(8,128)(2,1)} %pad_maximum_fusion.2), channel_id=1, source_target_pairs={{0,8},{8,16},{16,24},{1,9},{9,17},{17,25},{2,10},{10,18},{18,26},{... | collective-permute-start | bytes 3145736 | tf_op jit(solution)/shard_map/ppermute | solution.py:13
  24.8 11.8 copy-start.3
  36.6 11.8 copy-start.1
  61.7 11.8 copy-start.13
  86.1 85.0 %copy-start.38 = (f32[2048]{0:T(1024)S(1)}, f32[2048]{0:T(1024)}, u32[]{:S(2)}) copy-start(f32[2048]{0:T(1024)} %param.25) | copy-start | bytes 24580
  90.8 574.1 %all-reduce.8.cloned.1.call-start = ((), (), s32[]{:S(2)}) async-start(), calls=%async_computation.1 | async-start | bytes 8388608 | tf_op jit(solution)/shard_map/psum | solution.py:119
  204.9 13.3 collective-permute-start.1
  230.1 182.8 %collective-permute-start.2 = (f32[1024,2048]{1,0:T(8,128)}, f32[1024,2048]{1,0:T(8,128)}, u32[]{:S(2)}, u32[]{:S(2)}) collective-permute-start(f32[1024,2048]{1,0:T(8,128)} %add.222), channel_id=1, source_target_pairs={{0,2},{1,3},{2,0},{3,1},{4,6},{5,7},{6,4},{7,5},{8,10},{9,11},{10,... | collective-permute-start | bytes 25165832 | tf_op jit(solution)/shard_map/ppermute | solution.py:36
  424.7 226.9 %collective-permute-start.3 = (f32[1024,2048]{1,0:T(8,128)}, f32[1024,2048]{1,0:T(8,128)}, u32[]{:S(2)}, u32[]{:S(2)}) collective-permute-start(f32[1024,2048]{1,0:T(8,128)} %add.223), channel_id=1, source_target_pairs={{0,4},{1,5},{2,6},{3,7},{4,0},{5,1},{6,2},{7,3},{8,12},{9,13},{10,... | collective-permute-start | bytes 25165832 | tf_op jit(solution)/shard_map/ppermute | solution.py:36
  436.6 228.4 %copy-start.47 = (f32[2048]{0:T(1024)S(1)}, f32[2048]{0:T(1024)}, u32[]{:S(2)}) copy-start(f32[2048]{0:T(1024)} %param.31) | copy-start | bytes 24580
  436.6 1215.7 %all-reduce.10.cloned.1.call-start = ((), (), s32[]{:S(2)}) async-start(), calls=%async_computation.2 | async-start | bytes 50331648 | tf_op jit(solution)/shard_map/psum | solution.py:193
  665.0 13.9 copy-start.26
  706.2 15.6 copy-start.14
  740.8 14.2 slice-start.2
  744.0 11.0 slice-start.3
  744.0 11.0 copy-start.23
  744.0 48.4 %collective-permute-start.4 = (f32[2,1024,256]{2,1,0:T(8,128)}, f32[2,1024,256]{2,1,0:T(8,128)}, u32[]{:S(2)}, u32[]{:S(2)}) collective-permute-start(f32[2,1024,256]{2,1,0:T(8,128)} %fusion.29), channel_id=1, source_target_pairs={{8,0},{16,8},{24,16},{9,1},{17,9},{25,17},{10,2},{18,10},{26,18},{... | collective-permute-start | bytes 6291464 | tf_op jit(solution)/shard_map/ppermute | solution.py:13
  760.7 34.3 %copy-start.31 = (bf16[1024,1,256]{2,0,1:T(8,128)(2,1)S(1)}, bf16[1024,1,256]{2,0,1:T(8,128)(2,1)}, u32[]{:S(2)}) copy-start(bf16[1024,1,256]{2,0,1:T(8,128)(2,1)} %copy.47) | copy-start | bytes 1572868
  792.4 16.2 slice-start
  795.0 16.3 copy-start.34
  795.0 16.3 copy-start.36
  795.1 13.6 slice-start.1
  801.0 17.5 %collective-permute-start.5 = (f32[1024,2048]{1,0:T(8,128)}, f32[1024,2048]{1,0:T(8,128)}, u32[]{:S(2)}, u32[]{:S(2)}) collective-permute-start(f32[1024,2048]{1,0:T(8,128)} %convolution_bitcast_fusion), channel_id=1, source_target_pairs={{0,1},{1,0},{2,3},{3,2},{4,5},{5,4},{6,7},{7,6},{8,9},{9,8},{10,11... | collective-permute-start | bytes 25165832 | tf_op jit(solution)/shard_map/ppermute | solution.py:36
  831.4 196.4 %copy-start.32 = (bf16[1024,1,256]{2,0,1:T(8,128)(2,1)S(1)}, bf16[1024,1,256]{2,0,1:T(8,128)(2,1)}, u32[]{:S(2)}) copy-start(bf16[1024,1,256]{2,0,1:T(8,128)(2,1)} %copy.47) | copy-start | bytes 1572868
  831.4 196.4 %copy-start.35 = (bf16[1024,1,256]{2,0,1:T(8,128)(2,1)S(1)}, bf16[1024,1,256]{2,0,1:T(8,128)(2,1)}, u32[]{:S(2)}) copy-start(bf16[1024,1,256]{2,0,1:T(8,128)(2,1)} %copy-done.34) | copy-start | bytes 1572868
  831.4 196.4 %copy-start.37 = (bf16[1024,1,256]{2,0,1:T(8,128)(2,1)S(1)}, bf16[1024,1,256]{2,0,1:T(8,128)(2,1)}, u32[]{:S(2)}) copy-start(bf16[1024,1,256]{2,0,1:T(8,128)(2,1)} %copy-done.36) | copy-start | bytes 1572868
  831.4 183.3 %collective-permute-start.6 = (f32[1024,2048]{1,0:T(8,128)}, f32[1024,2048]{1,0:T(8,128)}, u32[]{:S(2)}, u32[]{:S(2)}) collective-permute-start(f32[1024,2048]{1,0:T(8,128)} %add.227), channel_id=1, source_target_pairs={{0,2},{1,3},{2,0},{3,1},{4,6},{5,7},{6,4},{7,5},{8,10},{9,11},{10,... | collective-permute-start | bytes 25165832 | tf_op jit(solution)/shard_map/ppermute | solution.py:36
  1026.6 182.3 %collective-permute-start.7 = (f32[1024,2048]{1,0:T(8,128)}, f32[1024,2048]{1,0:T(8,128)S(1)}, u32[]{:S(2)}, u32[]{:S(2)}) collective-permute-start(f32[1024,2048]{1,0:T(8,128)} %add.228), channel_id=1, source_target_pairs={{0,4},{1,5},{2,6},{3,7},{4,0},{5,1},{6,2},{7,3},{8,12},{9,13},{10,... | collective-permute-start | bytes 25165832 | tf_op jit(solution)/shard_map/ppermute | solution.py:36
  1028.1 190.8 %copy-start.48 = (f32[1024]{0:T(1024)S(1)}, f32[1024]{0:T(1024)}, u32[]{:S(2)}) copy-start(f32[1024]{0:T(1024)} %get-tuple-element.35) | copy-start | bytes 12292
  1652.3 8.9 copy-start.16
  (44 other events, 203.1 us)
Sparse Core Ops, SparseCore 0:
  91.0 80.0 all-reduce.5
  436.7 126.2 all-reduce.7
  818.6 833.6 all-reduce.9
